TPU v7x, 32 devices: a whole 2x2x4 slice. The times are simulated.
32 devices in a mesh: group: 4 (over y, x), space: 8 (over z, core).
Axes of the slice: x: 2, y: 2, z: 4, core: 2. Of those that a mesh axis runs over, the one named last changes fastest.
Arguments:
- vectors: bfloat16 [128, 2, 3, 4096], P('group', None, None, 'space'), may hold values from -3 to 3
- momentum: int32 [3], replicated, may hold values from -3 to 3
- assignment: int32 [128], replicated, may hold values from 0 to 127, each once
Outputs:
- elementals: float32 [128, 2, 128, 128], P('space', None, 'group')
Inputs may be any that keep to these rules, and one draw needn't show every extreme that they name: `assignment`: each eigenvector is named by exactly one slot.
All inputs are finite; a program needn't handle non-finite values.
Results may differ from a plain program's by a relative error of at most 0.0029.
Values may be sent and summed in bfloat16 or wider, within the bound.
A program may use at most 128 MiB of HBM per device.

v0:
```python
import math
import jax
import jax.numpy as jnp
from jax import lax
from jax.sharding import PartitionSpec as P

L = 64


def complex_product(left_re, left_im, right_re, right_im):
    return (left_re * right_re - left_im * right_im, left_re * right_im + left_im * right_re)


def weighted_slot(vec32, slot_vec, cosine, sine):
    crosses_re = []
    crosses_im = []
    for colour in range(3):
        second = (colour + 1) % 3
        third = (colour + 2) % 3
        one_re, one_im = complex_product(
            vec32[:, 0, second], vec32[:, 1, second], slot_vec[0, third], slot_vec[1, third]
        )
        two_re, two_im = complex_product(
            vec32[:, 0, third], vec32[:, 1, third], slot_vec[0, second], slot_vec[1, second]
        )
        cross_re = one_re - two_re
        cross_im = one_im - two_im
        crosses_re.append(cross_re * cosine - cross_im * sine)
        crosses_im.append(cross_re * sine + cross_im * cosine)
    stacked = jnp.stack([jnp.stack(crosses_re, axis=1), jnp.stack(crosses_im, axis=1)], axis=1)
    return stacked.astype(jnp.bfloat16)


def local(vectors, momentum, assignment):
    block_size = vectors.shape[0]
    site_count = vectors.shape[3]
    space_size = lax.axis_size("space")
    total_sites = site_count * space_size
    gathered = lax.all_gather(vectors, "group", axis=0, tiled=True)
    total_vecs = gathered.shape[0]
    sites = lax.axis_index("space") * site_count + jnp.arange(site_count, dtype=jnp.int32)
    coord_x = sites % L
    coord_y = sites // L % L
    coord_z = sites // (L * L)
    phase_index = jnp.mod(momentum[0] * coord_x + momentum[1] * coord_y + momentum[2] * coord_z, L)
    angle = phase_index.astype(jnp.float32) * jnp.float32(2.0 * math.pi / L)
    cosine = jnp.cos(angle)
    sine = jnp.sin(angle)
    slot_ids = lax.dynamic_slice_in_dim(
        assignment, lax.axis_index("group") * block_size, block_size
    )
    vec32 = gathered.astype(jnp.float32)

    def one_slot(index):
        slot_vec = jnp.take(vec32, index, axis=0)
        return weighted_slot(vec32, slot_vec, cosine, sine)

    weighted = lax.map(one_slot, slot_ids).reshape(block_size * total_vecs, 2, 3 * site_count)
    flat_left = gathered.reshape(total_vecs, 2, 3 * site_count)
    scale = jnp.float32(1.0 / math.sqrt(total_sites))
    row_count = total_vecs // space_size
    products = jnp.einsum("ipx,mqx->ipqm", flat_left, weighted, preferred_element_type=jnp.float32)
    real_part = products[:, 0, 0] - products[:, 1, 1]
    imag_part = products[:, 0, 1] + products[:, 1, 0]
    joined = jnp.stack([real_part, imag_part], axis=1)
    summed = lax.psum(joined.reshape(total_vecs, 2, block_size, total_vecs) * scale, "space")
    return lax.dynamic_slice_in_dim(summed, lax.axis_index("space") * row_count, row_count, 0)


def solution(mesh):
    placed = (P("group", None, None, "space"), P(), P())
    return jax.shard_map(
        local,
        mesh=mesh,
        in_specs=placed,
        out_specs=P("space", None, "group", None),
        check_vma=False,
    )
```

profile of v0, /device:TPU:0, one launch (start us, length us, event | category | flops | bytes accessed | tf_op | source)
XLA Modules:
  0.0 420.4 jit_solution(16571338819917680055)
XLA Ops:
  6.5 13.9 %all_gather.3 = bf16[128,2,3,512]{3,1,2,0:T(2,128)(2,1)S(1)} all-gather(bf16[32,2,3,512]{3,1,2,0:T(2,128)(2,1)} %param.5), channel_id=1, replica_groups=mesh['group'=4,'space'=8] {'group'}, dimensions={0}, use_global_device_ids=true | all-gather | bytes 983040 | tf_op jit(solution)/shard_map/all_gather | solution.py:39
  22.3 197.2 %while.13 = (s32[]{:T(128)}, bf16[32,128,2,3,512]{4,1,3,2,0:T(8,128)(2,1)}, f32[128,2,3,512]{3,0,2,1:T(8,128)S(1)}, s32[32]{0:T(128)S(1)}, s32[]{:T(128)}, /*ind...) while((s32[]{:T(128)}, ...), condition=%wide.region_1.2_spmd.clone.clone, body=%wide.region_0.1_spmd.clone.clone.sunk | while | flops 6717960 | bytes 9810637 | solution.py:58
  24.6 2.1 fusion.48
  30.8 2.1 fusion.48
  33.6 1.0 maximum_dynamic-update-slice_fusion.2
  36.9 2.1 fusion.48
  43.1 2.1 fusion.48
  49.2 2.1 fusion.48
  55.4 2.1 fusion.48
  58.2 1.0 maximum_dynamic-update-slice_fusion.2
  61.5 2.1 fusion.48
  64.3 1.0 maximum_dynamic-update-slice_fusion.2
  67.7 2.1 fusion.48
  73.8 2.1 fusion.48
  76.7 1.0 maximum_dynamic-update-slice_fusion.2
  80.0 2.1 fusion.48
  86.1 2.1 fusion.48
  89.0 1.1 maximum_dynamic-update-slice_fusion.2
  92.4 2.1 fusion.48
  95.2 1.1 maximum_dynamic-update-slice_fusion.2
  98.6 2.1 fusion.48
  104.7 2.1 fusion.48
  107.6 1.0 maximum_dynamic-update-slice_fusion.2
  110.9 2.1 fusion.48
  113.7 1.0 maximum_dynamic-update-slice_fusion.2
  117.1 2.1 fusion.48
  119.9 1.0 maximum_dynamic-update-slice_fusion.2
  123.2 2.1 fusion.48
  126.1 1.0 maximum_dynamic-update-slice_fusion.2
  129.4 2.1 fusion.48
  135.6 2.1 fusion.48
  138.4 1.0 maximum_dynamic-update-slice_fusion.2
  141.8 2.1 fusion.48
  144.6 1.0 maximum_dynamic-update-slice_fusion.2
  147.9 2.1 fusion.48
  150.7 1.0 maximum_dynamic-update-slice_fusion.2
  154.1 2.1 fusion.48
  156.9 1.0 maximum_dynamic-update-slice_fusion.2
  160.2 2.1 fusion.48
  163.1 1.0 maximum_dynamic-update-slice_fusion.2
  166.4 2.1 fusion.48
  169.2 1.0 maximum_dynamic-update-slice_fusion.2
  172.6 2.1 fusion.48
  178.7 2.1 fusion.48
  181.5 1.0 maximum_dynamic-update-slice_fusion.2
  184.8 2.1 fusion.48
  191.0 2.1 fusion.48
  193.8 1.0 maximum_dynamic-update-slice_fusion.2
  197.1 2.1 fusion.48
  200.0 1.0 maximum_dynamic-update-slice_fusion.2
  203.3 2.1 fusion.48
  206.1 1.0 maximum_dynamic-update-slice_fusion.2
  209.5 2.1 fusion.48
  215.6 2.1 fusion.48
  218.4 1.0 maximum_dynamic-update-slice_fusion.2
  219.5 33.5 %copy.33 = bf16[32,128,2,3,512]{1,0,4,3,2:T(8,128)(2,1)} copy(bf16[32,128,2,3,512]{4,1,3,2,0:T(8,128)(2,1)} %get-tuple-element.37) | data formatting | bytes 50331648 | tf_op jit(solution)/shard_map/while | solution.py:58
  253.0 37.4 %reshape.2091 = bf16[4096,2,1536,1]{0,2,3,1:T(8,128)(2,1)} reshape(bf16[32,128,2,3,512]{1,0,4,3,2:T(8,128)(2,1)} %copy.33) | data formatting | bytes 50331648 | tf_op jit(solution)/shard_map/reshape | solution.py:58
  290.3 12.7 %convolution_bitcast_fusion = f32[128,2,2,4096]{0,3,1,2:T(8,128)S(1)} fusion(bf16[4096,2,1536,1]{0,2,3,1:T(8,128)(2,1)} %reshape.2091, bf16[128,2,1536,1]{0,2,1,3:T(8,128)(2,1)S(1)} %bitcast.179), kind=kOutput, calls=%fused_computation.85 | convolution fusion | flops 6442450944 | bytes 34340864 | tf_op jit(solution)/shard_map/ipx,mqx->ipqm/dot_general | solution.py:62
  303.0 1.8 slice_subtract_fusion
  304.8 3.2 copy.37
  307.9 2.0 copy.38
  310.0 4.8 %maximum_multiply_fusion = f32[128,2,32,128]{3,2,1,0:T(8,128)} fusion(f32[128,1,32,128]{3,2,1,0:T(8,128)} %copy.38, f32[128,1,32,128]{3,2,1,0:T(8,128)} %copy.37), kind=kLoop, calls=%fused_computation.86 | loop fusion | flops 2097152 | bytes 8388608 | tf_op jit(solution)/shard_map/mul | solution.py:66
  314.8 96.9 %all-reduce.2.cloned.1.call-done = f32[128,2,32,128]{3,2,1,0:T(8,128)} async-done(((f32[128,2,32,128]{3,2,1,0:T(8,128)}), f32[128,2,32,128]{3,2,1,0:T(8,128)}) %all-reduce.2.cloned.1.call-update) | async-done | bytes 4194320 | tf_op jit(solution)/shard_map/psum | solution.py:66
  411.7 1.9 constant_dynamic-slice_fusion
  (310 shorter events, 55.4 us)
Async XLA Ops:
  6.5 15.0 %copy-start = (s32[3]{0:T(128)S(1)}, s32[3]{0:T(128)}, u32[]{:S(2)}) copy-start(s32[3]{0:T(128)} %param.6) | copy-start | bytes 40
  6.5 15.7 %copy-start.1 = (s32[128]{0:T(128)S(1)}, s32[128]{0:T(128)}, u32[]{:S(2)}) copy-start(s32[128]{0:T(128)} %param.7) | copy-start | bytes 1540
  6.5 405.2 %all-reduce.2.cloned.1.call-start = ((), (), s32[]{:S(2)}) async-start(), calls=%async_computation | async-start | bytes 8388608 | tf_op jit(solution)/shard_map/psum | solution.py:66
Sparse Core Ops, SparseCore 0:
  314.9 96.7 all-reduce.1
where the time goes:
time: 424 us; the launch traced here: 420 us
  other arithmetic  129 us (30%)
  local copies, waits for them, and re-layouts  98.1 us (23%)
  waiting for transfers between devices  97 us (23%)
  loops' own time  56.6 us (13%)
  blocking collectives  13.9 us (3%)
  between operations  13.4 us (3%)
  matrix products  12.7 us (3%)
    psum x1, waiting for transfers between devices, local(): lax.psum(joined.reshape(total_vecs, 2, block_size, total_vecs) * scale, '...  96.9 us
    sin x32, other arithmetic, local(): sine = jnp.sin(angle)  65.9 us
    another operation x1, loops' own time, local(): lax.map(one_slot, slot_ids)  56.6 us
    reshape x1, local copies, waits for them, and re-layouts, local(): lax.map(one_slot, slot_ids)  37.4 us
    while x1, local copies, waits for them, and re-layouts, local(): lax.map(one_slot, slot_ids)  33.5 us
    dynamic_update_slice x32, other arithmetic, local(): lax.map(one_slot, slot_ids)  31.7 us
    another operation x96, other arithmetic  20.9 us
    dynamic_slice x32, local copies, waits for them, and re-layouts, local(): lax.map(one_slot, slot_ids)  17.8 us
  transfers between devices with their start and end apart: 1, of which 1 were waited for; matrix products, arithmetic and copies ran while one was open for 0% of the time, Pallas kernels for 0%

commit v1 on v0

--- a/solution.py
+++ b/solution.py
@@ -5,6 +5,18 @@
 from jax.sharding import PartitionSpec as P
 
 L = 64
+
+
+def gather_by_bits(x, axis, dim):
+    ways, here, step = (lax.axis_size(axis), lax.axis_index(axis), x.shape[dim])
+    line, have = (x, 1)
+    while have < ways:
+        line = jnp.concatenate(
+            [line, lax.ppermute(line, axis, [(d, (d - have) % ways) for d in range(ways)])],
+            axis=dim,
+        )
+        have = 2 * have
+    return jnp.roll(line, here * step, axis=dim)
 
 
 def complex_product(left_re, left_im, right_re, right_im):
@@ -36,7 +48,7 @@
     site_count = vectors.shape[3]
     space_size = lax.axis_size("space")
     total_sites = site_count * space_size
-    gathered = lax.all_gather(vectors, "group", axis=0, tiled=True)
+    gathered = gather_by_bits(vectors, "group", 0)
     total_vecs = gathered.shape[0]
     sites = lax.axis_index("space") * site_count + jnp.arange(site_count, dtype=jnp.int32)
     coord_x = sites % L

time: 424 us -> 440 us (1.038)
  blocking collectives: 13.9 us -> 0 us
  waiting for transfers between devices: 97 us -> 108 us
  local copies, waits for them, and re-layouts: 98.1 us -> 109 us
  starting transfers between devices: 0.01 us -> 5.57 us
  loops' own time: 56.6 us -> 61.5 us
    all_gather x1 -> x0, blocking collectives: 13.9 us -> none  [local(): gathered = lax.all_gather(vectors, 'group', axis=0, tiled=True)]
    ppermute x0 -> x2, waiting for transfers between devices: none -> 8.81 us  [gather_by_bits(): lax.ppermute(line, axis, [(d, (d - have) % ways) for d in range(ways)])]
    ppermute x0 -> x2, starting transfers between devices: none -> 5.57 us  [gather_by_bits(): lax.ppermute(line, axis, [(d, (d - have) % ways) for d in range(ways)])]
    another operation x1, loops' own time: 56.6 us -> 61.5 us  [local(): lax.map(one_slot, slot_ids)]
  transfers between devices with their start and end apart: 1 -> 3, of which waited for: 1 -> 3; matrix products, arithmetic and copies ran while one was open for 0% -> 1% of each run, Pallas kernels for 0% -> 0%
where the time goes in v1:
time: 440 us; the launch traced here: 436 us
  other arithmetic  126 us (29%)
  local copies, waits for them, and re-layouts  109 us (25%)
  waiting for transfers between devices  108 us (25%)
  loops' own time  61.5 us (14%)
  between operations  13.5 us (3%)
  matrix products  12.7 us (3%)
  starting transfers between devices  5.57 us (1%)
    psum x1, waiting for transfers between devices, local(): lax.psum(joined.reshape(total_vecs, 2, block_size, total_vecs) * scale, '...  99 us
    sin x32, other arithmetic, local(): sine = jnp.sin(angle)  63 us
    another operation x1, loops' own time, local(): lax.map(one_slot, slot_ids)  61.5 us
    reshape x1, local copies, waits for them, and re-layouts, local(): lax.map(one_slot, slot_ids)  37.4 us
    while x1, local copies, waits for them, and re-layouts, local(): lax.map(one_slot, slot_ids)  33.5 us
    dynamic_update_slice x32, other arithmetic, local(): lax.map(one_slot, slot_ids)  31.7 us
    another operation x96, other arithmetic  20.9 us
    dynamic_slice x32, local copies, waits for them, and re-layouts, local(): lax.map(one_slot, slot_ids)  20.3 us
  transfers between devices with their start and end apart: 3, of which 3 were waited for; matrix products, arithmetic and copies ran while one was open for 1% of the time, Pallas kernels for 0%

profile of v1, /device:TPU:0, one launch (start us, length us, event | category | flops | bytes accessed | tf_op | source)
XLA Modules:
  0.0 436.1 jit_solution(4805674354528777546)
XLA Ops:
  7.5 3.9 collective-permute-start
  11.4 4.2 collective-permute-done
  15.6 1.6 collective-permute-start.1
  17.3 1.3 copy.52
  19.3 1.4 fusion.43
  21.1 4.7 %collective-permute-done.1 = bf16[64,2,3,512]{3,0,2,1:T(8,128)(2,1)S(1)} collective-permute-done((bf16[64,2,3,512]{3,0,2,1:T(8,128)(2,1)S(1)}, bf16[64,2,3,512]{3,0,2,1:T(8,128)(2,1)S(1)}, u32[]{:S(2)}, u32[]{:S(2)}) %collective-permute-start.1) | collective-permute-done | bytes 393248 | tf_op jit(solution)/shard_map/ppermute | solution.py:15
  26.2 3.4 concatenate.20
  29.6 1.4 constant_dynamic-slice_fusion.1
  31.3 201.7 %while.13 = (s32[]{:T(128)}, bf16[32,128,2,3,512]{4,1,3,2,0:T(8,128)(2,1)}, f32[128,2,3,512]{3,0,2,1:T(8,128)S(1)}, s32[32]{0:T(128)S(1)}, s32[]{:T(128)}, /*ind...) while((s32[]{:T(128)}, ...), condition=%wide.region_1.2_spmd.clone.clone, body=%wide.region_0.1_spmd.clone.clone.sunk | while | flops 6717960 | bytes 9810637 | solution.py:70
  33.9 2.0 fusion.48
  40.2 2.0 fusion.48
  42.9 1.0 maximum_dynamic-update-slice_fusion.2
  46.5 2.0 fusion.48
  52.7 2.0 fusion.48
  59.0 2.0 fusion.48
  65.3 2.0 fusion.48
  71.6 2.0 fusion.48
  74.4 1.0 maximum_dynamic-update-slice_fusion.2
  77.9 2.0 fusion.48
  84.2 2.0 fusion.48
  90.5 2.0 fusion.48
  96.8 2.0 fusion.48
  99.5 1.1 maximum_dynamic-update-slice_fusion.2
  103.2 2.0 fusion.48
  105.9 1.1 maximum_dynamic-update-slice_fusion.2
  109.6 2.0 fusion.48
  115.8 2.0 fusion.48
  118.6 1.0 maximum_dynamic-update-slice_fusion.2
  122.1 2.0 fusion.48
  128.4 2.0 fusion.48
  131.2 1.0 maximum_dynamic-update-slice_fusion.2
  134.8 2.0 fusion.48
  137.5 1.0 maximum_dynamic-update-slice_fusion.2
  141.1 2.0 fusion.48
  147.4 2.0 fusion.48
  150.1 1.0 maximum_dynamic-update-slice_fusion.2
  153.7 2.0 fusion.48
  156.4 1.0 maximum_dynamic-update-slice_fusion.2
  160.0 2.0 fusion.48
  162.7 1.0 maximum_dynamic-update-slice_fusion.2
  166.3 2.0 fusion.48
  172.6 2.0 fusion.48
  178.9 2.0 fusion.48
  181.6 1.0 maximum_dynamic-update-slice_fusion.2
  185.2 2.0 fusion.48
  191.5 2.0 fusion.48
  197.8 2.0 fusion.48
  204.0 2.0 fusion.48
  210.3 2.0 fusion.48
  213.1 1.0 maximum_dynamic-update-slice_fusion.2
  216.6 2.0 fusion.48
  219.4 1.0 maximum_dynamic-update-slice_fusion.2
  222.9 2.0 fusion.48
  229.2 2.0 fusion.48
  232.0 1.0 maximum_dynamic-update-slice_fusion.2
  233.0 33.5 %copy.59 = bf16[32,128,2,3,512]{1,0,4,3,2:T(8,128)(2,1)} copy(bf16[32,128,2,3,512]{4,1,3,2,0:T(8,128)(2,1)} %get-tuple-element.37) | data formatting | bytes 50331648 | tf_op jit(solution)/shard_map/while | solution.py:70
  266.5 37.4 %reshape.2091 = bf16[4096,2,1536,1]{0,2,3,1:T(8,128)(2,1)} reshape(bf16[32,128,2,3,512]{1,0,4,3,2:T(8,128)(2,1)} %copy.59) | data formatting | bytes 50331648 | tf_op jit(solution)/shard_map/reshape | solution.py:70
  303.9 12.7 %convolution_bitcast_fusion = f32[128,2,2,4096]{0,3,1,2:T(8,128)S(1)} fusion(bf16[4096,2,1536,1]{0,2,3,1:T(8,128)(2,1)} %reshape.2091, bf16[128,2,1536,1]{0,2,1,3:T(8,128)(2,1)S(1)} %bitcast.178), kind=kOutput, calls=%fused_computation.85 | convolution fusion | flops 6442450944 | bytes 34340864 | tf_op jit(solution)/shard_map/ipx,mqx->ipqm/dot_general | solution.py:74
  316.6 1.8 slice_subtract_fusion
  318.3 3.2 copy.62
  321.5 2.0 copy.63
  323.5 4.8 %maximum_multiply_fusion = f32[128,2,32,128]{3,2,1,0:T(8,128)} fusion(f32[128,1,32,128]{3,2,1,0:T(8,128)} %copy.63, f32[128,1,32,128]{3,2,1,0:T(8,128)} %copy.62), kind=kLoop, calls=%fused_computation.86 | loop fusion | flops 2097152 | bytes 8388608 | tf_op jit(solution)/shard_map/mul | solution.py:78
  328.3 99.0 %all-reduce.2.cloned.1.call-done = f32[128,2,32,128]{3,2,1,0:T(8,128)} async-done(((f32[128,2,32,128]{3,2,1,0:T(8,128)}), f32[128,2,32,128]{3,2,1,0:T(8,128)}) %all-reduce.2.cloned.1.call-update) | async-done | bytes 4194320 | tf_op jit(solution)/shard_map/psum | solution.py:78
  427.4 1.9 constant_dynamic-slice_fusion
  (315 shorter events, 65.8 us)
Async XLA Ops:
  6.5 420.8 %all-reduce.2.cloned.1.call-start = ((), (), s32[]{:S(2)}) async-start(), calls=%async_computation | async-start | bytes 8388608 | tf_op jit(solution)/shard_map/psum | solution.py:78
  7.5 8.1 %collective-permute-start = (bf16[32,2,3,512]{3,0,2,1:T(8,128)(2,1)S(1)}, bf16[32,2,3,512]{3,0,2,1:T(8,128)(2,1)S(1)}, u32[]{:S(2)}, u32[]{:S(2)}) collective-permute-start(bf16[32,2,3,512]{3,0,2,1:T(8,128)(2,1)S(1)} %copy.50), channel_id=1, source_target_pairs={{0,24},{8,0},{16,8},{24,16},{1,25},{9,1},{17,9},{25,17},{2,26},{10... | collective-permute-start | bytes 589832 | tf_op jit(solution)/shard_map/ppermute | solution.py:15
  15.6 10.2 %collective-permute-start.1 = (bf16[64,2,3,512]{3,0,2,1:T(8,128)(2,1)S(1)}, bf16[64,2,3,512]{3,0,2,1:T(8,128)(2,1)S(1)}, u32[]{:S(2)}, u32[]{:S(2)}) collective-permute-start(bf16[64,2,3,512]{3,0,2,1:T(8,128)(2,1)S(1)} %pad_maximum_fusion), channel_id=1, source_target_pairs={{0,16},{8,24},{16,0},{24,8},{1,17},{9,25},{17,1},{25,9},{2,18},{10... | collective-permute-start | bytes 1179656 | tf_op jit(solution)/shard_map/ppermute | solution.py:15
Sparse Core Ops, SparseCore 0:
  328.4 98.8 all-reduce.1

commit v2 on v0

--- a/solution.py
+++ b/solution.py
@@ -63,7 +63,10 @@
     real_part = products[:, 0, 0] - products[:, 1, 1]
     imag_part = products[:, 0, 1] + products[:, 1, 0]
     joined = jnp.stack([real_part, imag_part], axis=1)
-    summed = lax.psum(joined.reshape(total_vecs, 2, block_size, total_vecs) * scale, "space")
+    summed = jnp.sum(
+        lax.all_gather(joined.reshape(total_vecs, 2, block_size, total_vecs) * scale, "space"),
+        axis=0,
+    )
     return lax.dynamic_slice_in_dim(summed, lax.axis_index("space") * row_count, row_count, 0)
 
 

time: 424 us -> 631 us (1.49)
  waiting for transfers between devices: 97 us -> 289 us
  other arithmetic: 129 us -> 144 us
    all_gather x0 -> x1, waiting for transfers between devices: none -> 289 us  [local(): lax.all_gather(joined.reshape(total_vecs, 2, block_size, total_vecs) * sc...]
    psum x1 -> x0, waiting for transfers between devices: 96.9 us -> none  [local(): lax.psum(joined.reshape(total_vecs, 2, block_size, total_vecs) * scale, '...]
    reduce_sum x0 -> x1, other arithmetic: none -> 15.2 us  [local(): jnp.sum(lax.all_gather(joined.reshape(total_vecs, 2, block_size, total_ve...]
where the time goes in v2:
time: 631 us; the launch traced here: 628 us
  waiting for transfers between devices  289 us (46%)
  other arithmetic  144 us (23%)
  local copies, waits for them, and re-layouts  98.1 us (16%)
  loops' own time  56.6 us (9%)
  blocking collectives  13.9 us (2%)
  between operations  13.4 us (2%)
  matrix products  12.7 us (2%)
    all_gather x1, waiting for transfers between devices, local(): lax.all_gather(joined.reshape(total_vecs, 2, block_size, total_vecs) * sc...  289 us
    sin x32, other arithmetic, local(): sine = jnp.sin(angle)  65.9 us
    another operation x1, loops' own time, local(): lax.map(one_slot, slot_ids)  56.6 us
    reshape x1, local copies, waits for them, and re-layouts, local(): lax.map(one_slot, slot_ids)  37.4 us
    while x1, local copies, waits for them, and re-layouts, local(): lax.map(one_slot, slot_ids)  33.5 us
    dynamic_update_slice x32, other arithmetic, local(): lax.map(one_slot, slot_ids)  31.7 us
    another operation x96, other arithmetic  20.9 us
    dynamic_slice x32, local copies, waits for them, and re-layouts, local(): lax.map(one_slot, slot_ids)  17.8 us
  transfers between devices with their start and end apart: 1, of which 1 were waited for; matrix products, arithmetic and copies ran while one was open for 0% of the time, Pallas kernels for 0%

profile of v2, /device:TPU:0, one launch (start us, length us, event | category | flops | bytes accessed | tf_op | source)
XLA Modules:
  0.0 627.8 jit_solution(8605753754241394115)
XLA Ops:
  6.5 13.9 %all_gather.7 = bf16[128,2,3,512]{3,1,2,0:T(2,128)(2,1)S(1)} all-gather(bf16[32,2,3,512]{3,1,2,0:T(2,128)(2,1)} %param.5), channel_id=1, replica_groups=mesh['group'=4,'space'=8] {'group'}, dimensions={0}, use_global_device_ids=true | all-gather | bytes 983040 | tf_op jit(solution)/shard_map/all_gather | solution.py:39
  22.3 197.2 %while.13 = (s32[]{:T(128)}, bf16[32,128,2,3,512]{4,1,3,2,0:T(8,128)(2,1)}, f32[128,2,3,512]{3,0,2,1:T(8,128)S(1)}, s32[32]{0:T(128)S(1)}, s32[]{:T(128)}, /*ind...) while((s32[]{:T(128)}, ...), condition=%wide.region_1.2_spmd.clone.clone, body=%wide.region_0.1_spmd.clone.clone.sunk | while | flops 6717960 | bytes 9810637 | solution.py:58
  24.6 2.1 fusion.48
  30.8 2.1 fusion.48
  33.6 1.0 maximum_dynamic-update-slice_fusion.2
  36.9 2.1 fusion.48
  43.1 2.1 fusion.48
  49.2 2.1 fusion.48
  55.4 2.1 fusion.48
  58.2 1.0 maximum_dynamic-update-slice_fusion.2
  61.5 2.1 fusion.48
  64.3 1.0 maximum_dynamic-update-slice_fusion.2
  67.7 2.1 fusion.48
  73.8 2.1 fusion.48
  76.7 1.0 maximum_dynamic-update-slice_fusion.2
  80.0 2.1 fusion.48
  86.1 2.1 fusion.48
  89.0 1.1 maximum_dynamic-update-slice_fusion.2
  92.4 2.1 fusion.48
  95.2 1.1 maximum_dynamic-update-slice_fusion.2
  98.6 2.1 fusion.48
  104.7 2.1 fusion.48
  107.6 1.0 maximum_dynamic-update-slice_fusion.2
  110.9 2.1 fusion.48
  113.7 1.0 maximum_dynamic-update-slice_fusion.2
  117.1 2.1 fusion.48
  119.9 1.0 maximum_dynamic-update-slice_fusion.2
  123.2 2.1 fusion.48
  126.1 1.0 maximum_dynamic-update-slice_fusion.2
  129.4 2.1 fusion.48
  135.6 2.1 fusion.48
  138.4 1.0 maximum_dynamic-update-slice_fusion.2
  141.8 2.1 fusion.48
  144.6 1.0 maximum_dynamic-update-slice_fusion.2
  147.9 2.1 fusion.48
  150.7 1.0 maximum_dynamic-update-slice_fusion.2
  154.1 2.1 fusion.48
  156.9 1.0 maximum_dynamic-update-slice_fusion.2
  160.2 2.1 fusion.48
  163.1 1.0 maximum_dynamic-update-slice_fusion.2
  166.4 2.1 fusion.48
  169.2 1.0 maximum_dynamic-update-slice_fusion.2
  172.6 2.1 fusion.48
  178.7 2.1 fusion.48
  181.5 1.0 maximum_dynamic-update-slice_fusion.2
  184.8 2.1 fusion.48
  191.0 2.1 fusion.48
  197.1 2.1 fusion.48
  200.0 1.0 maximum_dynamic-update-slice_fusion.2
  203.3 2.1 fusion.48
  206.1 1.0 maximum_dynamic-update-slice_fusion.2
  209.5 2.1 fusion.48
  215.6 2.1 fusion.48
  218.4 1.0 maximum_dynamic-update-slice_fusion.2
  219.5 33.5 %copy.33 = bf16[32,128,2,3,512]{1,0,4,3,2:T(8,128)(2,1)} copy(bf16[32,128,2,3,512]{4,1,3,2,0:T(8,128)(2,1)} %get-tuple-element.37) | data formatting | bytes 50331648 | tf_op jit(solution)/shard_map/while | solution.py:58
  253.0 37.4 %reshape.2134 = bf16[4096,2,1536,1]{0,2,3,1:T(8,128)(2,1)} reshape(bf16[32,128,2,3,512]{1,0,4,3,2:T(8,128)(2,1)} %copy.33) | data formatting | bytes 50331648 | tf_op jit(solution)/shard_map/reshape | solution.py:58
  290.3 12.7 %convolution_bitcast_fusion = f32[128,2,2,4096]{0,3,1,2:T(8,128)S(1)} fusion(bf16[4096,2,1536,1]{0,2,3,1:T(8,128)(2,1)} %reshape.2134, bf16[128,2,1536,1]{0,2,1,3:T(8,128)(2,1)S(1)} %bitcast.179), kind=kOutput, calls=%fused_computation.85 | convolution fusion | flops 6442450944 | bytes 34340864 | tf_op jit(solution)/shard_map/ipx,mqx->ipqm/dot_general | solution.py:62
  303.0 1.7 slice_subtract_fusion
  304.8 3.1 copy.37
  307.9 2.0 copy.38
  309.9 4.9 maximum_multiply_fusion
  314.8 289.0 %all-gather.2.cloned.1.call-done = f32[8,128,2,32,128]{4,3,2,1,0:T(8,128)} async-done(((f32[1,128,2,32,128]{4,3,2,1,0:T(8,128)}), f32[8,128,2,32,128]{4,3,2,1,0:T(8,128)}) %all-gather.2.cloned.1.call-update) | async-done | bytes 33554448 | tf_op jit(solution)/shard_map/all_gather | solution.py:67
  603.9 15.2 %reduce_sum.9 = f32[128,2,32,128]{3,2,1,0:T(8,128)} reduce(f32[8,128,2,32,128]{4,3,2,1,0:T(8,128)} %all-gather.2.cloned.1.call-done, f32[]{:T(128)} %constant.95.clone.1), dimensions={0}, to_apply=%region_2.3 | reduce | flops 7340032 | bytes 37748740 | tf_op jit(solution)/shard_map/reduce_sum | solution.py:66
  619.0 1.9 constant_dynamic-slice_fusion
  (311 shorter events, 56.4 us)
Async XLA Ops:
  6.5 15.0 %copy-start = (s32[3]{0:T(128)S(1)}, s32[3]{0:T(128)}, u32[]{:S(2)}) copy-start(s32[3]{0:T(128)} %param.6) | copy-start | bytes 40
  6.5 15.7 %copy-start.1 = (s32[128]{0:T(128)S(1)}, s32[128]{0:T(128)}, u32[]{:S(2)}) copy-start(s32[128]{0:T(128)} %param.7) | copy-start | bytes 1540
  6.5 597.3 %all-gather.2.cloned.1.call-start = ((), (), s32[]{:S(2)}) async-start(), calls=%async_computation | async-start | bytes 37748736 | tf_op jit(solution)/shard_map/all_gather | solution.py:67
Sparse Core Ops, SparseCore 0:
  315.0 288.8 all-gather.1
